TPU v7x, 32 devices: a whole 2x2x4 slice. The times are simulated.
32 devices in a mesh: groups: 2 (over y), seq: 4 (over z), segment: 2 (over x), owner: 2 (over core).
Axes of the slice: x: 2, y: 2, z: 4, core: 2. Of those that a mesh axis runs over, the one named last changes fastest.
Arguments:
- layer_input_rows: bfloat16 [2, 512, 5376], P('segment', ('groups', 'seq')), parts along dimension 1, may hold values from -40 to 40
- encoded_query_rows: bfloat16 [2, 512, 2048], P('segment', ('groups', 'seq'), 'owner'), parts along dimension 1, may hold values from -213 to 213
- encoded_key_rows: bfloat16 [2, 512, 1024], P('segment', ('groups', 'seq'), 'owner'), parts along dimension 1, may hold values from -6 to 6
- layer_norm_gain: float32 [2, 5376], P('segment'), may hold values from 0.25 to 1.75
- base_value_matrix: bfloat16 [2, 5376, 1024], P('segment', ('seq', 'owner')), may hold values from -0.078125 to 0.078125
- adapter_down_panels: bfloat16 [2, 8, 5376, 64], P('segment', 'seq', 'owner'), may hold values from -0.078125 to 0.078125
- adapter_up_panels: bfloat16 [2, 8, 64, 1024], P('segment', 'seq', None, 'owner'), may hold values from -0.75 to 0.75
- request_token_lengths: int32 [8], P('groups'), parts along dimension 0, may hold values from 1 to 128, 256 in all
- adapter_per_request: int32 [8], P('groups'), parts along dimension 0, may hold values from 0 to 7
- rank_per_adapter: int32 [8], replicated, may hold values from 16 to 64
- slot_per_adapter: int32 [8], replicated, may hold values from 0 to 7, each once
Outputs:
- layer_output: bfloat16 [2, 512, 2048], P('segment', ('groups', 'seq'), 'owner'), parts along dimension 1
There are 2 independent parts, one for each index of `groups`. A program takes and returns all parts, laid end to end along the dimension named above; an argument that names none is the same for every part. Nothing has to cross between parts.
All inputs are finite; a program needn't handle non-finite values.
Results may differ from a plain program's by a relative error of at most 0.0065.
Values may be sent and summed in bfloat16 or wider, within the bound.
A program may use at most 128 MiB of HBM per device.

v0:
```python
import jax
import jax.numpy as jnp
from jax import lax
from jax.sharding import PartitionSpec as P

WINDOW = 1024
HEADS = 16
KEY_VALUE_HEADS = 8
HEAD_SIZE = 128
query_scale = 168.0 ** (-0.5)
adapter_strength = 32.0
norm_eps = 1e-06


def broadcast(x, axis, root):
    mine = lax.axis_index(axis) == root
    return lax.psum(jnp.where(mine, x, jnp.zeros_like(x)), axis)


def from_behind(value, axis, steps):
    count = lax.axis_size(axis)
    first, last = (max(0, -steps), min(count, count - steps))
    return lax.ppermute(value, axis, [(source, source + steps) for source in range(first, last)])


def per_device(
    layer_input_rows,
    encoded_query_rows,
    encoded_key_rows,
    layer_norm_gain,
    base_value_matrix,
    adapter_down_panels,
    adapter_up_panels,
    request_token_lengths,
    adapter_per_request,
    rank_per_adapter,
    slot_per_adapter,
):
    hidden = layer_input_rows[0]
    row_count = hidden.shape[0]
    seq_now = lax.axis_index("seq")
    owner_now = lax.axis_index("owner")
    reach_count = min(WINDOW // row_count, lax.axis_size("seq") - 1)
    requests = request_token_lengths.shape[0]
    library = slot_per_adapter.shape[0]
    slots_here = adapter_down_panels.shape[1]
    rows_halved = adapter_down_panels.shape[2]
    rank_span_width = adapter_down_panels.shape[3]
    key_value_halved = adapter_up_panels.shape[3]
    group_size = HEADS // KEY_VALUE_HEADS
    request_ends = jnp.cumsum(request_token_lengths)
    position = seq_now * row_count + jnp.arange(row_count, dtype=jnp.int32)
    context = seq_now * row_count + jnp.arange(-reach_count * row_count, row_count, dtype=jnp.int32)
    request_lookup = jnp.sum((position[:, None] >= request_ends[None, :]).astype(jnp.int32), axis=1)
    request_ctx = jnp.sum((context[:, None] >= request_ends[None, :]).astype(jnp.int32), axis=1)
    live_mask = (context[None, :] <= position[:, None]) & (
        context[None, :] > position[:, None] - WINDOW
    )
    live_mask = (
        live_mask & (context[None, :] >= 0) & (request_ctx[None, :] == request_lookup[:, None])
    )
    choose = adapter_per_request[:, None] == jnp.arange(library, dtype=jnp.int32)[None, :]
    slot_of = jnp.sum(jnp.where(choose, slot_per_adapter[None, :], 0), axis=1)
    rank_lookup = jnp.sum(jnp.where(choose, rank_per_adapter[None, :], 0), axis=1)
    scale_lookup = adapter_strength / rank_lookup.astype(jnp.float32)
    in_request = request_lookup[:, None] == jnp.arange(requests, dtype=jnp.int32)[None, :]
    column_live = jnp.arange(rank_span_width, dtype=jnp.int32)[None, :] < rank_lookup[:, None]
    row_gain_weight = jnp.where(in_request, scale_lookup[None, :], jnp.float32(0.0))
    down_panel_here = adapter_down_panels[0]
    up_panel_here = adapter_up_panels[0]
    queries = encoded_query_rows[0]
    keys_own = encoded_key_rows[0]
    key_heads = keys_own.shape[1] // HEAD_SIZE
    wide_rows = hidden.astype(jnp.float32)
    normalized_rows = wide_rows * lax.rsqrt(
        jnp.mean(wide_rows * wide_rows, axis=1, keepdims=True) + norm_eps
    )
    normalized_rows = (normalized_rows * layer_norm_gain[0][None, :]).astype(jnp.bfloat16)
    normed_half = lax.dynamic_slice_in_dim(normalized_rows, owner_now * rows_halved, rows_halved, 1)
    full_value = jnp.dot(
        normalized_rows,
        lax.all_gather(base_value_matrix[0], ("seq", "owner"), axis=0, tiled=True),
        preferred_element_type=jnp.float32,
    )
    value_base_rows = lax.dynamic_slice_in_dim(
        full_value, owner_now * key_value_halved, key_value_halved, 1
    )

    def fetch_one(reduced_rows, request_index):
        owner_slot = slot_of[request_index]
        holder = owner_slot // slots_here
        local_slot = owner_slot % slots_here
        down_local = lax.dynamic_slice_in_dim(down_panel_here, local_slot, 1, 0)
        up_local = lax.dynamic_slice_in_dim(up_panel_here, local_slot, 1, 0)
        down_piece, up_piece = (
            broadcast(down_local, "seq", holder),
            broadcast(up_local, "seq", holder),
        )
        keep_mask = in_request[:, request_index][:, None] & column_live[request_index][None, :]
        matrix_product = jnp.dot(normed_half, down_piece[0], preferred_element_type=jnp.float32)
        return (reduced_rows + jnp.where(keep_mask, matrix_product, jnp.float32(0.0)), up_piece[0])

    start_low = jnp.zeros((row_count, rank_span_width), jnp.float32)
    reduced_rows, panels_up = lax.scan(fetch_one, start_low, jnp.arange(requests, dtype=jnp.int32))
    reduced_rows = lax.psum(reduced_rows, "owner").astype(jnp.bfloat16)
    raised_rows = jnp.einsum(
        "tr,qrk->qtk", reduced_rows, panels_up, preferred_element_type=jnp.float32
    )
    adapter_value = jnp.sum(row_gain_weight.T[:, :, None] * raised_rows, axis=0)
    value_output_rows = (value_base_rows + adapter_value).astype(jnp.bfloat16)
    key_parts = []
    value_parts = []
    for shift_by in range(reach_count, 0, -1):
        key_piece, value_piece = from_behind((keys_own, value_output_rows), "seq", shift_by)
        key_parts.append(key_piece)
        value_parts.append(value_piece)
    keys_all = jnp.concatenate(key_parts + [keys_own], axis=0)
    values_all = jnp.concatenate(value_parts + [value_output_rows], axis=0)
    query_view = queries.reshape(row_count, key_heads, group_size, HEAD_SIZE)
    key_view = keys_all.reshape(-1, key_heads, HEAD_SIZE)
    value_view = values_all.reshape(-1, key_heads, HEAD_SIZE)
    head_outputs = []
    for head_index in range(key_heads):
        query_head = query_view[:, head_index]
        scores = (
            jnp.einsum(
                "tcd,jd->ctj",
                query_head,
                key_view[:, head_index],
                preferred_element_type=jnp.float32,
            )
            * query_scale
        )
        scores = jnp.where(live_mask[None], scores, jnp.float32(-1e30))
        row_max = jnp.max(scores, axis=-1, keepdims=True)
        weights = jnp.exp(scores - row_max)
        row_total = jnp.sum(weights, axis=-1, keepdims=True)
        softmax_rows = (weights / row_total).astype(jnp.bfloat16)
        mixed = jnp.einsum(
            "ctj,jd->tcd",
            softmax_rows,
            value_view[:, head_index],
            preferred_element_type=jnp.float32,
        )
        head_outputs.append(mixed.astype(jnp.bfloat16).reshape(row_count, group_size * HEAD_SIZE))
    result = jnp.concatenate(head_outputs, axis=1)
    return result[None]


def solution(mesh):
    in_specs = (
        P("segment", ("groups", "seq"), None),
        P("segment", ("groups", "seq"), "owner"),
        P("segment", ("groups", "seq"), "owner"),
        P("segment", None),
        P("segment", ("seq", "owner"), None),
        P("segment", "seq", "owner", None),
        P("segment", "seq", None, "owner"),
        P("groups"),
        P("groups"),
        P(),
        P(),
    )
    out_specs = P("segment", ("groups", "seq"), "owner")
    return jax.shard_map(
        per_device, mesh=mesh, in_specs=in_specs, out_specs=out_specs, check_vma=False
    )
```

profile of v0, /device:TPU:0, one launch (start us, length us, event | category | flops | bytes accessed | tf_op | source)
XLA Modules:
  0.0 353.9 jit_solution(13641821148216391470)
XLA Ops:
  7.4 1.4 fusion.8
  10.7 1.7 copy.36
  13.4 211.6 %while.15 = (s32[]{:T(128)}, f32[64,64]{0,1:T(8,128)S(1)}, bf16[4,64,512]{2,1,0:T(8,128)(2,1)S(1)}, s32[4]{0:T(128)S(1)}, pred[64,4]{0,1:T(4,128)(4,1)S(1)}, /*i...) while((s32[]{:T(128)}, f32[64,64]{0,1:T(8,128)S(1)}, ...), condition=%wide.region_8.9_spmd.clone, body=%wide.region_5.8_spmd.clone.sunk | while | flops 22446112 | bytes 4817837 | solution.py:104
  19.1 0.9 select_bitcast_fusion.2
  20.7 45.7 %all-reduce.5.cloned.1.call-done = (bf16[2688,64]{1,0:T(8,128)(2,1)}, bf16[1,64,512]{2,1,0:T(8,128)(2,1)}) async-done(((bf16[2688,64]{1,0:T(8,128)(2,1)}, bf16[1,64,512]{2,1,0:T(8,128)(2,1)}), (bf16[2688,64]{1,0:T(8,128)(2,1)}, bf16[1,64,512]{2,1,0:T(8,128)(2,1)})) %all-reduce.5.cloned.1.call-update) | async-done | bytes 409616 | tf_op jit(solution)/shard_map/while/body/eval_jaxpr/psum | solution.py:17
  67.2 1.5 fusion.74
  74.5 0.9 select_bitcast_fusion.2
  76.1 42.3 %all-reduce.5.cloned.1.call-done = (bf16[2688,64]{1,0:T(8,128)(2,1)}, bf16[1,64,512]{2,1,0:T(8,128)(2,1)}) async-done(((bf16[2688,64]{1,0:T(8,128)(2,1)}, bf16[1,64,512]{2,1,0:T(8,128)(2,1)}), (bf16[2688,64]{1,0:T(8,128)(2,1)}, bf16[1,64,512]{2,1,0:T(8,128)(2,1)})) %all-reduce.5.cloned.1.call-update) | async-done | bytes 409616 | tf_op jit(solution)/shard_map/while/body/eval_jaxpr/psum | solution.py:17
  119.3 1.5 fusion.74
  126.6 0.9 select_bitcast_fusion.2
  128.2 42.3 %all-reduce.5.cloned.1.call-done = (bf16[2688,64]{1,0:T(8,128)(2,1)}, bf16[1,64,512]{2,1,0:T(8,128)(2,1)}) async-done(((bf16[2688,64]{1,0:T(8,128)(2,1)}, bf16[1,64,512]{2,1,0:T(8,128)(2,1)}), (bf16[2688,64]{1,0:T(8,128)(2,1)}, bf16[1,64,512]{2,1,0:T(8,128)(2,1)})) %all-reduce.5.cloned.1.call-update) | async-done | bytes 409616 | tf_op jit(solution)/shard_map/while/body/eval_jaxpr/psum | solution.py:17
  171.4 1.5 fusion.74
  180.3 42.3 %all-reduce.5.cloned.1.call-done = (bf16[2688,64]{1,0:T(8,128)(2,1)}, bf16[1,64,512]{2,1,0:T(8,128)(2,1)}) async-done(((bf16[2688,64]{1,0:T(8,128)(2,1)}, bf16[1,64,512]{2,1,0:T(8,128)(2,1)}), (bf16[2688,64]{1,0:T(8,128)(2,1)}, bf16[1,64,512]{2,1,0:T(8,128)(2,1)})) %all-reduce.5.cloned.1.call-update) | async-done | bytes 409616 | tf_op jit(solution)/shard_map/while/body/eval_jaxpr/psum | solution.py:17
  223.4 1.5 fusion.74
  225.8 3.7 %collective-permute-start.3 = (bf16[64,512]{1,0:T(8,128)(2,1)S(1)}, bf16[64,512]{1,0:T(8,128)(2,1)S(1)}, u32[]{:S(2)}, u32[]{:S(2)}) collective-permute-start(bf16[64,512]{1,0:T(8,128)(2,1)S(1)} %bitcast.212), channel_id=1, source_target_pairs={{0,12},{1,13},{2,14},{3,15},{16,28},{17,29},{18,30},{19,31}} | collective-permute-start | bytes 196616 | tf_op jit(solution)/shard_map/ppermute | solution.py:23
  229.5 1.3 collective-permute-start.4
  230.8 2.5 collective-permute-start.5
  233.5 3.4 psum.27
  239.3 90.8 %all-gather.3.cloned.1.call-done = bf16[1,5376,1024]{2,1,0:T(8,128)(2,1)} async-done(((bf16[1,672,1024]{2,1,0:T(8,128)(2,1)}), bf16[1,5376,1024]{2,1,0:T(8,128)(2,1)}) %all-gather.3.cloned.1.call-update) | async-done | bytes 11010064 | tf_op jit(solution)/shard_map/all_gather | solution.py:82
  330.1 6.1 %fusion.6 = f32[64,1024]{1,0:T(8,128)S(1)} fusion(bf16[64,5376]{1,0:T(8,128)(2,1)S(1)} %fusion.10, bf16[1,5376,1024]{2,1,0:T(8,128)(2,1)} %all-gather.3.cloned.1.call-done), kind=kOutput, calls=%fused_computation.12 | convolution fusion | flops 704643072 | bytes 11960320 | tf_op jit(solution)/shard_map/dot_general | solution.py:80
  336.3 2.3 collective-permute-start
  338.6 1.3 collective-permute-start.1
  339.9 2.5 collective-permute-start.2
  342.7 1.5 collective-permute-done.2
  (99 shorter events, 20.7 us)
Async XLA Ops:
  7.4 5.1 %copy-start.4 = (f32[1,5376]{1,0:T(1,128)S(1)}, f32[1,5376]{1,0:T(1,128)}, u32[]{:S(2)}) copy-start(f32[1,5376]{1,0:T(1,128)} %param.16) | copy-start | bytes 64516
  7.4 5.2 %copy-start = (bf16[1,64,5376]{2,1,0:T(8,128)(2,1)S(1)}, bf16[1,64,5376]{2,1,0:T(8,128)(2,1)}, u32[]{:S(2)}) copy-start(bf16[1,64,5376]{2,1,0:T(8,128)(2,1)} %param.13) | copy-start | bytes 2064388
  12.5 0.9 copy-start.1
  13.4 53.0 %all-reduce.5.cloned.1.call-start = ((), (), s32[]{:S(2)}) async-start(), calls=%async_computation.1 | async-start | bytes 1507328 | tf_op jit(solution)/shard_map/while/body/eval_jaxpr/psum | solution.py:17
  68.7 49.7 %all-reduce.5.cloned.1.call-start = ((), (), s32[]{:S(2)}) async-start(), calls=%async_computation.1 | async-start | bytes 1507328 | tf_op jit(solution)/shard_map/while/body/eval_jaxpr/psum | solution.py:17
  120.8 49.7 %all-reduce.5.cloned.1.call-start = ((), (), s32[]{:S(2)}) async-start(), calls=%async_computation.1 | async-start | bytes 1507328 | tf_op jit(solution)/shard_map/while/body/eval_jaxpr/psum | solution.py:17
  172.9 49.7 %all-reduce.5.cloned.1.call-start = ((), (), s32[]{:S(2)}) async-start(), calls=%async_computation.1 | async-start | bytes 1507328 | tf_op jit(solution)/shard_map/while/body/eval_jaxpr/psum | solution.py:17
  224.9 0.8 copy-start.3
  225.0 8.4 %copy-start.2 = (bf16[1,64,1024]{2,1,0:T(8,128)(2,1)S(1)}, bf16[1,64,1024]{2,1,0:T(8,128)(2,1)}, u32[]{:S(2)}) copy-start(bf16[1,64,1024]{2,1,0:T(8,128)(2,1)} %param.14) | copy-start | bytes 393220
  225.0 105.1 %all-gather.3.cloned.1.call-start = ((), (), s32[]{:S(2)}) async-start(), calls=%async_computation | async-start | bytes 12386304 | tf_op jit(solution)/shard_map/all_gather | solution.py:82
  225.8 11.7 %collective-permute-start.3 = (bf16[64,512]{1,0:T(8,128)(2,1)S(1)}, bf16[64,512]{1,0:T(8,128)(2,1)S(1)}, u32[]{:S(2)}, u32[]{:S(2)}) collective-permute-start(bf16[64,512]{1,0:T(8,128)(2,1)S(1)} %bitcast.212), channel_id=1, source_target_pairs={{0,12},{1,13},{2,14},{3,15},{16,28},{17,29},{18,30},{19,31}} | collective-permute-start | bytes 196616 | tf_op jit(solution)/shard_map/ppermute | solution.py:23
  229.5 8.0 %collective-permute-start.4 = (bf16[64,512]{1,0:T(8,128)(2,1)S(1)}, bf16[64,512]{1,0:T(8,128)(2,1)S(1)}, u32[]{:S(2)}, u32[]{:S(2)}) collective-permute-start(bf16[64,512]{1,0:T(8,128)(2,1)S(1)} %bitcast.213), channel_id=1, source_target_pairs={{0,8},{4,12},{1,9},{5,13},{2,10},{6,14},{3,11},{7,15},{16,24},{20,... | collective-permute-start | bytes 196616 | tf_op jit(solution)/shard_map/ppermute | solution.py:23
  230.8 6.8 %collective-permute-start.5 = (bf16[64,512]{1,0:T(8,128)(2,1)S(1)}, bf16[64,512]{1,0:T(8,128)(2,1)S(1)}, u32[]{:S(2)}, u32[]{:S(2)}) collective-permute-start(bf16[64,512]{1,0:T(8,128)(2,1)S(1)} %bitcast.214), channel_id=1, source_target_pairs={{0,4},{4,8},{8,12},{1,5},{5,9},{9,13},{2,6},{6,10},{10,14},{3,7},{... | collective-permute-start | bytes 196616 | tf_op jit(solution)/shard_map/ppermute | solution.py:23
  336.3 6.4 %collective-permute-start = (bf16[64,512]{1,0:T(8,128)(2,1)S(1)}, bf16[64,512]{1,0:T(8,128)(2,1)S(1)}, u32[]{:S(2)}, u32[]{:S(2)}) collective-permute-start(bf16[64,512]{1,0:T(8,128)(2,1)S(1)} %fusion.32), channel_id=1, source_target_pairs={{0,12},{1,13},{2,14},{3,15},{16,28},{17,29},{18,30},{19,31}} | collective-permute-start | bytes 196616 | tf_op jit(solution)/shard_map/ppermute | solution.py:23
  338.6 4.1 %collective-permute-start.1 = (bf16[64,512]{1,0:T(8,128)(2,1)S(1)}, bf16[64,512]{1,0:T(8,128)(2,1)S(1)}, u32[]{:S(2)}, u32[]{:S(2)}) collective-permute-start(bf16[64,512]{1,0:T(8,128)(2,1)S(1)} %fusion.32), channel_id=1, source_target_pairs={{0,8},{4,12},{1,9},{5,13},{2,10},{6,14},{3,11},{7,15},{16,24},{20,... | collective-permute-start | bytes 196616 | tf_op jit(solution)/shard_map/ppermute | solution.py:23
  339.9 4.4 %collective-permute-start.2 = (bf16[64,512]{1,0:T(8,128)(2,1)S(1)}, bf16[64,512]{1,0:T(8,128)(2,1)S(1)}, u32[]{:S(2)}, u32[]{:S(2)}) collective-permute-start(bf16[64,512]{1,0:T(8,128)(2,1)S(1)} %fusion.32), channel_id=1, source_target_pairs={{0,4},{4,8},{8,12},{1,5},{5,9},{9,13},{2,6},{6,10},{10,14},{3,7},{... | collective-permute-start | bytes 196616 | tf_op jit(solution)/shard_map/ppermute | solution.py:23
Sparse Core Ops, SparseCore 0:
  20.8 45.5 all-reduce.4
  76.2 42.1 all-reduce.4
  128.3 42.1 all-reduce.4
  180.4 42.1 all-reduce.4
Sparse Core Ops, SparseCore 1:
  227.1 103.0 all-gather.2
where the time goes:
time: 355 us; the launch traced here: 354 us
  waiting for transfers between devices  266 us (75%)
  loops' own time  18.5 us (5%)
  matrix products  15.6 us (4%)
  between operations  14.9 us (4%)
  starting transfers between devices  13.7 us (4%)
  local copies, waits for them, and re-layouts  11.6 us (3%)
  other arithmetic  10.8 us (3%)
    psum x4, waiting for transfers between devices, broadcast(): return lax.psum(jnp.where(mine, x, jnp.zeros_like(x)), axis)  173 us
    all_gather x1, waiting for transfers between devices, per_device(): lax.all_gather(base_value_matrix[0], ('seq', 'owner'), axis=0, tiled=True)  90.8 us
    another operation x1, loops' own time, per_device(): lax.scan(fetch_one, start_low, jnp.arange(requests, dtype=jnp.int32))  18.5 us
    ppermute x6, starting transfers between devices, from_behind(): lax.ppermute(value, axis, [(source, source + steps) for source in range(f...  13.5 us
  transfers between devices with their start and end apart: 11, of which 6 were waited for; matrix products, arithmetic and copies ran while one was open for 1% of the time, Pallas kernels for 0%

commit v1 on v0

--- a/solution.py
+++ b/solution.py
@@ -14,7 +14,7 @@
 
 def broadcast(x, axis, root):
     mine = lax.axis_index(axis) == root
-    return lax.psum(jnp.where(mine, x, jnp.zeros_like(x)), axis)
+    return jnp.sum(lax.all_gather(jnp.where(mine, x, jnp.zeros_like(x)), axis), axis=0)
 
 
 def from_behind(value, axis, steps):

time: 355 us -> 316 us (0.89)
  waiting for transfers between devices: 266 us -> 169 us
  blocking collectives: 3.43 us -> 65.9 us
  local copies, waits for them, and re-layouts: 11.6 us -> 5.95 us
  other arithmetic: 10.8 us -> 16 us
  matrix products: 15.6 us -> 10.6 us
    psum x4 -> x0, waiting for transfers between devices: 173 us -> none  [broadcast(): return lax.psum(jnp.where(mine, x, jnp.zeros_like(x)), axis)]
    all_gather x0 -> x4, waiting for transfers between devices: none -> 76.1 us  [broadcast(): lax.all_gather(jnp.where(mine, x, jnp.zeros_like(x)), axis)]
    all_gather x0 -> x4, blocking collectives: none -> 62.5 us  [broadcast(): lax.all_gather(jnp.where(mine, x, jnp.zeros_like(x)), axis)]
    reduce_sum x0 -> x8, other arithmetic: none -> 6.4 us  [broadcast(): jnp.sum(lax.all_gather(jnp.where(mine, x, jnp.zeros_like(x)), axis), axis=0)]
    dot_general x4, matrix products: 5.97 us -> 0.95 us  [fetch_one(): jnp.dot(normed_half, down_piece[0], preferred_element_type=jnp.float32)]
    squeeze x4 -> x0, other arithmetic: 3.62 us -> none  [fetch_one(): down_piece[0]]
where the time goes in v1:
time: 316 us; the launch traced here: 315 us
  waiting for transfers between devices  169 us (53%)
  blocking collectives  65.9 us (21%)
  loops' own time  18.6 us (6%)
  other arithmetic  16 us (5%)
  between operations  14.9 us (5%)
  starting transfers between devices  13.8 us (4%)
  matrix products  10.6 us (3%)
  local copies, waits for them, and re-layouts  5.95 us (2%)
    all_gather x1, waiting for transfers between devices, per_device(): lax.all_gather(base_value_matrix[0], ('seq', 'owner'), axis=0, tiled=True)  90.7 us
    all_gather x4, waiting for transfers between devices, broadcast(): lax.all_gather(jnp.where(mine, x, jnp.zeros_like(x)), axis)  76.1 us
    all_gather x4, blocking collectives, broadcast(): lax.all_gather(jnp.where(mine, x, jnp.zeros_like(x)), axis)  62.5 us
    another operation x1, loops' own time, per_device(): lax.scan(fetch_one, start_low, jnp.arange(requests, dtype=jnp.int32))  18.6 us
    ppermute x6, starting transfers between devices, from_behind(): lax.ppermute(value, axis, [(source, source + steps) for source in range(f...  13.6 us
    reduce_sum x8, other arithmetic, broadcast(): jnp.sum(lax.all_gather(jnp.where(mine, x, jnp.zeros_like(x)), axis), axis=0)  6.4 us
  transfers between devices with their start and end apart: 11, of which 6 were waited for; matrix products, arithmetic and copies ran while one was open for 1% of the time, Pallas kernels for 0%

profile of v1, /device:TPU:0, one launch (start us, length us, event | category | flops | bytes accessed | tf_op | source)
XLA Modules:
  0.0 314.7 jit_solution(11571302662901535599)
XLA Ops:
  7.4 1.4 fusion.8
  11.5 1.3 fusion.10
  12.9 172.8 %while.16 = (s32[]{:T(128)}, f32[64,64]{0,1:T(8,128)S(1)}, bf16[4,64,512]{2,1,0:T(8,128)(2,1)S(1)}, s32[4]{0:T(128)S(1)}, pred[64,4]{0,1:T(4,128)(4,1)S(1)}, /*i...) while((s32[]{:T(128)}, f32[64,64]{0,1:T(8,128)S(1)}, ...), condition=%wide.region_8.9_spmd.clone, body=%wide.region_5.8_spmd.clone.sunk | while | flops 22855712 | bytes 9208761 | solution.py:104
  19.5 16.7 %all-gather.8 = bf16[4,64,512]{2,1,0:T(8,128)(2,1)S(1)} all-gather(bf16[1,64,512]{2,1,0:T(8,128)(2,1)S(1)} %dynamic-slice_select_fusion.5), channel_id=3, replica_groups=mesh['groups'=2,'seq'=4,'segment'=2,'owner'=2] {'seq'}, dimensions={0}, use_global_device_ids=true | all-gather | bytes 327680 | tf_op jit(solution)/shard_map/while/body/eval_jaxpr/all_gather | solution.py:17
  36.3 20.6 %all-gather.14.cloned.1.call-done = bf16[4,2688,64]{1,2,0:T(8,128)(2,1)} async-done(((bf16[1,2688,64]{1,2,0:T(8,128)(2,1)}), bf16[4,2688,64]{1,2,0:T(8,128)(2,1)}) %all-gather.14.cloned.1.call-update) | async-done | bytes 1376272 | tf_op jit(solution)/shard_map/while/body/eval_jaxpr/all_gather | solution.py:17
  56.9 1.6 reduce.22
  65.3 15.4 %all-gather.8 = bf16[4,64,512]{2,1,0:T(8,128)(2,1)S(1)} all-gather(bf16[1,64,512]{2,1,0:T(8,128)(2,1)S(1)} %dynamic-slice_select_fusion.5), channel_id=3, replica_groups=mesh['groups'=2,'seq'=4,'segment'=2,'owner'=2] {'seq'}, dimensions={0}, use_global_device_ids=true | all-gather | bytes 327680 | tf_op jit(solution)/shard_map/while/body/eval_jaxpr/all_gather | solution.py:17
  80.9 18.2 %all-gather.14.cloned.1.call-done = bf16[4,2688,64]{1,2,0:T(8,128)(2,1)} async-done(((bf16[1,2688,64]{1,2,0:T(8,128)(2,1)}), bf16[4,2688,64]{1,2,0:T(8,128)(2,1)}) %all-gather.14.cloned.1.call-update) | async-done | bytes 1376272 | tf_op jit(solution)/shard_map/while/body/eval_jaxpr/all_gather | solution.py:17
  99.1 1.6 reduce.22
  107.5 15.0 %all-gather.8 = bf16[4,64,512]{2,1,0:T(8,128)(2,1)S(1)} all-gather(bf16[1,64,512]{2,1,0:T(8,128)(2,1)S(1)} %dynamic-slice_select_fusion.5), channel_id=3, replica_groups=mesh['groups'=2,'seq'=4,'segment'=2,'owner'=2] {'seq'}, dimensions={0}, use_global_device_ids=true | all-gather | bytes 327680 | tf_op jit(solution)/shard_map/while/body/eval_jaxpr/all_gather | solution.py:17
  122.6 18.9 %all-gather.14.cloned.1.call-done = bf16[4,2688,64]{1,2,0:T(8,128)(2,1)} async-done(((bf16[1,2688,64]{1,2,0:T(8,128)(2,1)}), bf16[4,2688,64]{1,2,0:T(8,128)(2,1)}) %all-gather.14.cloned.1.call-update) | async-done | bytes 1376272 | tf_op jit(solution)/shard_map/while/body/eval_jaxpr/all_gather | solution.py:17
  141.6 1.6 reduce.22
  150.0 15.3 %all-gather.8 = bf16[4,64,512]{2,1,0:T(8,128)(2,1)S(1)} all-gather(bf16[1,64,512]{2,1,0:T(8,128)(2,1)S(1)} %dynamic-slice_select_fusion.5), channel_id=3, replica_groups=mesh['groups'=2,'seq'=4,'segment'=2,'owner'=2] {'seq'}, dimensions={0}, use_global_device_ids=true | all-gather | bytes 327680 | tf_op jit(solution)/shard_map/while/body/eval_jaxpr/all_gather | solution.py:17
  165.4 18.4 %all-gather.14.cloned.1.call-done = bf16[4,2688,64]{1,2,0:T(8,128)(2,1)} async-done(((bf16[1,2688,64]{1,2,0:T(8,128)(2,1)}), bf16[4,2688,64]{1,2,0:T(8,128)(2,1)}) %all-gather.14.cloned.1.call-update) | async-done | bytes 1376272 | tf_op jit(solution)/shard_map/while/body/eval_jaxpr/all_gather | solution.py:17
  183.9 1.6 reduce.22
  186.5 3.8 %collective-permute-start.3 = (bf16[64,512]{1,0:T(8,128)(2,1)S(1)}, bf16[64,512]{1,0:T(8,128)(2,1)S(1)}, u32[]{:S(2)}, u32[]{:S(2)}) collective-permute-start(bf16[64,512]{1,0:T(8,128)(2,1)S(1)} %bitcast.212), channel_id=1, source_target_pairs={{0,12},{1,13},{2,14},{3,15},{16,28},{17,29},{18,30},{19,31}} | collective-permute-start | bytes 196616 | tf_op jit(solution)/shard_map/ppermute | solution.py:23
  190.3 1.3 collective-permute-start.4
  191.6 2.5 collective-permute-start.5
  194.3 3.4 %psum.7 = bf16[64,64]{1,0:T(8,128)(2,1)S(1)} all-reduce(f32[64,64]{1,0:T(8,128)S(1)} %copy.70), channel_id=1, replica_groups=mesh['groups'=2,'seq'=4,'segment'=2,'owner'=2] {'owner'}, use_global_device_ids=true, to_apply=%region_9.10 | all-reduce | flops 4096 | bytes 24576 | tf_op jit(solution)/shard_map/psum | solution.py:105
  200.2 90.7 %all-gather.12.cloned.1.call-done = bf16[1,5376,1024]{2,1,0:T(8,128)(2,1)} async-done(((bf16[1,672,1024]{2,1,0:T(8,128)(2,1)}), bf16[1,5376,1024]{2,1,0:T(8,128)(2,1)}) %all-gather.12.cloned.1.call-update) | async-done | bytes 11010064 | tf_op jit(solution)/shard_map/all_gather | solution.py:82
  290.9 6.1 %fusion.6 = f32[64,1024]{1,0:T(8,128)S(1)} fusion(bf16[64,5376]{1,0:T(8,128)(2,1)S(1)} %fusion.10, bf16[1,5376,1024]{2,1,0:T(8,128)(2,1)} %all-gather.12.cloned.1.call-done), kind=kOutput, calls=%fused_computation.12 | convolution fusion | flops 704643072 | bytes 11960320 | tf_op jit(solution)/shard_map/dot_general | solution.py:80
  297.1 2.3 collective-permute-start
  300.7 2.5 collective-permute-start.2
  303.5 1.5 collective-permute-done.2
  (108 shorter events, 19.5 us)
Async XLA Ops:
  7.4 5.5 %copy-start = (bf16[1,2,2688,64]{2,3,1,0:T(8,128)(2,1)S(1)}, bf16[1,2,2688,64]{2,3,1,0:T(8,128)(2,1)}, u32[]{:S(2)}) copy-start(bf16[1,2,2688,64]{2,3,1,0:T(8,128)(2,1)} %param.18) | copy-start | bytes 2064388
  7.4 5.5 %copy-start.1 = (bf16[1,2,64,512]{3,2,1,0:T(8,128)(2,1)S(1)}, bf16[1,2,64,512]{3,2,1,0:T(8,128)(2,1)}, u32[]{:S(2)}) copy-start(bf16[1,2,64,512]{3,2,1,0:T(8,128)(2,1)} %param.19) | copy-start | bytes 393220
  12.9 44.0 %all-gather.14.cloned.1.call-start = ((), (), s32[]{:S(2)}) async-start(), calls=%async_computation.1 | async-start | bytes 1720320 | tf_op jit(solution)/shard_map/while/body/eval_jaxpr/all_gather | solution.py:17
  58.7 40.3 %all-gather.14.cloned.1.call-start = ((), (), s32[]{:S(2)}) async-start(), calls=%async_computation.1 | async-start | bytes 1720320 | tf_op jit(solution)/shard_map/while/body/eval_jaxpr/all_gather | solution.py:17
  100.9 40.7 %all-gather.14.cloned.1.call-start = ((), (), s32[]{:S(2)}) async-start(), calls=%async_computation.1 | async-start | bytes 1720320 | tf_op jit(solution)/shard_map/while/body/eval_jaxpr/all_gather | solution.py:17
  143.4 40.5 %all-gather.14.cloned.1.call-start = ((), (), s32[]{:S(2)}) async-start(), calls=%async_computation.1 | async-start | bytes 1720320 | tf_op jit(solution)/shard_map/while/body/eval_jaxpr/all_gather | solution.py:17
  185.7 0.8 copy-start.3
  185.7 8.5 %copy-start.2 = (bf16[1,64,1024]{2,1,0:T(8,128)(2,1)S(1)}, bf16[1,64,1024]{2,1,0:T(8,128)(2,1)}, u32[]{:S(2)}) copy-start(bf16[1,64,1024]{2,1,0:T(8,128)(2,1)} %param.14) | copy-start | bytes 393220
  185.7 105.2 %all-gather.12.cloned.1.call-start = ((), (), s32[]{:S(2)}) async-start(), calls=%async_computation | async-start | bytes 12386304 | tf_op jit(solution)/shard_map/all_gather | solution.py:82
  186.5 11.8 %collective-permute-start.3 = (bf16[64,512]{1,0:T(8,128)(2,1)S(1)}, bf16[64,512]{1,0:T(8,128)(2,1)S(1)}, u32[]{:S(2)}, u32[]{:S(2)}) collective-permute-start(bf16[64,512]{1,0:T(8,128)(2,1)S(1)} %bitcast.212), channel_id=1, source_target_pairs={{0,12},{1,13},{2,14},{3,15},{16,28},{17,29},{18,30},{19,31}} | collective-permute-start | bytes 196616 | tf_op jit(solution)/shard_map/ppermute | solution.py:23
  190.3 8.1 %collective-permute-start.4 = (bf16[64,512]{1,0:T(8,128)(2,1)S(1)}, bf16[64,512]{1,0:T(8,128)(2,1)S(1)}, u32[]{:S(2)}, u32[]{:S(2)}) collective-permute-start(bf16[64,512]{1,0:T(8,128)(2,1)S(1)} %bitcast.213), channel_id=1, source_target_pairs={{0,8},{4,12},{1,9},{5,13},{2,10},{6,14},{3,11},{7,15},{16,24},{20,... | collective-permute-start | bytes 196616 | tf_op jit(solution)/shard_map/ppermute | solution.py:23
  191.6 6.8 %collective-permute-start.5 = (bf16[64,512]{1,0:T(8,128)(2,1)S(1)}, bf16[64,512]{1,0:T(8,128)(2,1)S(1)}, u32[]{:S(2)}, u32[]{:S(2)}) collective-permute-start(bf16[64,512]{1,0:T(8,128)(2,1)S(1)} %bitcast.214), channel_id=1, source_target_pairs={{0,4},{4,8},{8,12},{1,5},{5,9},{9,13},{2,6},{6,10},{10,14},{3,7},{... | collective-permute-start | bytes 196616 | tf_op jit(solution)/shard_map/ppermute | solution.py:23
  297.1 6.4 %collective-permute-start = (bf16[64,512]{1,0:T(8,128)(2,1)S(1)}, bf16[64,512]{1,0:T(8,128)(2,1)S(1)}, u32[]{:S(2)}, u32[]{:S(2)}) collective-permute-start(bf16[64,512]{1,0:T(8,128)(2,1)S(1)} %fusion.32), channel_id=1, source_target_pairs={{0,12},{1,13},{2,14},{3,15},{16,28},{17,29},{18,30},{19,31}} | collective-permute-start | bytes 196616 | tf_op jit(solution)/shard_map/ppermute | solution.py:23
  299.4 4.1 %collective-permute-start.1 = (bf16[64,512]{1,0:T(8,128)(2,1)S(1)}, bf16[64,512]{1,0:T(8,128)(2,1)S(1)}, u32[]{:S(2)}, u32[]{:S(2)}) collective-permute-start(bf16[64,512]{1,0:T(8,128)(2,1)S(1)} %fusion.32), channel_id=1, source_target_pairs={{0,8},{4,12},{1,9},{5,13},{2,10},{6,14},{3,11},{7,15},{16,24},{20,... | collective-permute-start | bytes 196616 | tf_op jit(solution)/shard_map/ppermute | solution.py:23
  300.7 4.4 %collective-permute-start.2 = (bf16[64,512]{1,0:T(8,128)(2,1)S(1)}, bf16[64,512]{1,0:T(8,128)(2,1)S(1)}, u32[]{:S(2)}, u32[]{:S(2)}) collective-permute-start(bf16[64,512]{1,0:T(8,128)(2,1)S(1)} %fusion.32), channel_id=1, source_target_pairs={{0,4},{4,8},{8,12},{1,5},{5,9},{9,13},{2,6},{6,10},{10,14},{3,7},{... | collective-permute-start | bytes 196616 | tf_op jit(solution)/shard_map/ppermute | solution.py:23
Sparse Core Ops, SparseCore 0:
  19.6 37.2 all-gather.13
  65.4 33.5 all-gather.13
  107.6 33.9 all-gather.13
  150.1 33.7 all-gather.13
Sparse Core Ops, SparseCore 1:
  187.8 103.0 all-gather.11
